TPU v7x, 32 devices: a whole 2x2x4 slice. The times are simulated.
32 devices in a mesh: row: 4 (over y, core), col: 8 (over z, x).
Axes of the slice: x: 2, y: 2, z: 4, core: 2. Of those that a mesh axis runs over, the one named last changes fastest.
Arguments:
- precip: float32 [1024, 4096], P('row', 'col'), may hold values from 0.002 to 0.02
- head: float32 [1024, 4096], P('row', 'col'), may hold values from -4 to 4
- trans_coef: float32 [1024, 4096], P('row', 'col'), may hold values from 0.05 to 0.5
- land: int32 [1024, 4096], P('row', 'col'), may hold values 0 or 1
- dest: int32 [1024, 32], P('row', 'col'), may hold values from 0 to 32767, as said below
- moisture: float32 [32768, 16, 128], P(('row', 'col')), may hold values from 0.08 to 0.42
- ksat: float32 [32768, 128], P(('row', 'col')), may hold values from 0.002 to 0.01
Outputs:
- saturation: float32 [32768, 16, 128], P(('row', 'col'))
- head_new: float32 [1024, 4096], P('row', 'col')
Inputs may be any that keep to these rules, and one draw needn't show every extreme that they name: dest is a permutation of 0 .. 32767; its value is an owner's index along row+col times 1024 plus a slot. At most 64 blocks of one device's tile go to one owner, and every device sends exactly 64 to some owner; every owner receives 1024 blocks.
All inputs are finite; a program needn't handle non-finite values. No bound on the sum of `land` on one device may be relied on, other than what follows from the above.
Results may differ from a plain program's by a relative error of at most 0.00002.
Values sent between devices are 32-bit elements; how exact they have to be, the bound alone decides.
A program may use at most 192 MiB of HBM per device.

v0:
```python
import functools
import math

import jax
import jax.numpy as jnp
from jax import lax
from jax.experimental import pallas as pl
from jax.experimental.pallas import tpu as pltpu
from jax.sharding import PartitionSpec as P

SWEEPS = 4
LANES = 128

layer_depth = 0.1
step_ratio = 0.1
residual_water = 0.05
pore_range = 0.4
diff_length = 0.5
couple_rate = 0.05
recharge_gain = 20.0
store_rate = 0.2

VM = pl.BlockSpec(memory_space=pltpu.VMEM)
SM = pl.BlockSpec(memory_space=pltpu.SMEM)


def f32(*shape):
    return jax.ShapeDtypeStruct(shape, jnp.float32)


def pack_kernel(peers, per_peer, src, labels, precip, head, land, out, infil, heads):
    rows, cols = precip.shape
    for j in range(cols // LANES):
        part = pl.ds(j * LANES, LANES)
        infil[pl.ds(j * rows, rows), :] = precip[:, part] * land[:, part].astype(jnp.float32)
        heads[pl.ds(j * rows, rows), :] = head[:, part]

    def body(p, _):
        for r in range(per_peer):
            block = src[p * per_peer + r]
            out[p, pl.ds(r, 1), :] = infil[pl.ds(block, 1), :]
            out[p, pl.ds(per_peer + r, 1), :] = heads[pl.ds(block, 1), :]
        out[p, pl.ds(2 * per_peer, 8), :] = jnp.broadcast_to(labels[pl.ds(p, 1), :], (8, LANES))
        return 0

    lax.fori_loop(0, peers, body, 0)


def owner_kernel(
    peers, per_peer, slots, arrived, rec0, rec_x, rec_y, answer, infil, sig, own_i, own_h, rec
):
    owned = rec0.shape[0]

    def scatter(p, _):
        for r in range(per_peer):
            slot = slots[p * per_peer + r]
            own_i[pl.ds(slot, 1), :] = arrived[p, pl.ds(r, 1), :]
            own_h[pl.ds(slot, 1), :] = arrived[p, pl.ds(per_peer + r, 1), :]
        return 0

    lax.fori_loop(0, peers, scatter, 0)
    rec[pl.ds(owned, 8), :] = jnp.zeros((8, LANES), jnp.float32)

    def combine(g, _):
        part = pl.ds(g * 64, 64)
        inf = own_i[part, :]
        sg = jax.nn.sigmoid(own_h[part, :])
        infil[part, :] = inf
        sig[part, :] = sg
        rec[part, :] = rec0[part, :] + inf * rec_x[part, :] + sg * rec_y[part, :]
        return 0

    lax.fori_loop(0, owned // 64, combine, 0)

    def gather(p, _):
        for r in range(per_peer):
            slot = slots[p * per_peer + r]
            answer[p, pl.ds(r, 1), :] = rec[pl.ds(slot, 1), :]
        return 0

    lax.fori_loop(0, peers, gather, 0)


def factor_kernel(layers, group, moist, ksat, s0, sx, sy, rec0, rec_x, rec_y):
    count = ksat.shape[0]

    def body(step, _):
        base_row = step * group
        rows = pl.ds(pl.multiple_of(base_row, group), group)
        ks = ksat[rows, :]
        ratios, reds, xs = [], [], []
        before = None
        for k in range(layers):
            m = moist[pl.ds(base_row * layers + k, group, stride=layers), :]
            w = (m - residual_water) * (1.0 / pore_range)
            s = ks * math.exp(-(k + 0.5) * layer_depth)
            sw2 = s * (w * w)
            hs = sw2 * (1.5 / pore_range)
            d = s * (0.2 * diff_length / (2.0 * layer_depth)) + sw2 * (
                diff_length / (2.0 * layer_depth)
            )
            hc = 0.5 * (sw2 * w)
            cur = (m, hs, d, hc)
            if before is None:
                before = cur
                g_up = q_up = nsub = None
                continue
            m0, hs0, d0, hc0 = before
            g = d0 + d
            q = (hc0 + hc) - g * (m - m0)
            if g_up is None:
                pivot = step_ratio + g + hs0
                inv = 1.0 / pivot
                reds.append(-q * inv)
                xs.append(inv)
            else:
                pivot = step_ratio + g_up + g - nsub * ratios[-1]
                inv = 1.0 / pivot
                reds.append(((q_up - q) + nsub * reds[-1]) * inv)
                xs.append(nsub * inv * xs[-1])
            ratios.append((g - hs) * inv)
            nsub = hs0 + g
            g_up, q_up = g, q
            before = cur
        m, hs, d, hc = before
        bottom = 2.0 * hc + couple_rate * (m - residual_water)
        pivot = step_ratio + g_up + hs + couple_rate - nsub * ratios[-1]
        inv = 1.0 / pivot
        change = ((q_up - bottom) + nsub * reds[-1]) * inv
        cx = nsub * inv * xs[-1]
        cy = (couple_rate * pore_range) * inv
        gain = 2.0 * hs + couple_rate
        rec0[rows, :] = bottom + gain * change
        rec_x[rows, :] = gain * cx
        rec_y[rows, :] = gain * cy - couple_rate * pore_range
        unit = 1.0 / pore_range
        for k in range(layers - 1, -1, -1):
            if k < layers - 1:
                change = reds[k] + ratios[k] * change
                cx = xs[k] + ratios[k] * cx
                cy = ratios[k] * cy
            m = moist[pl.ds(base_row * layers + k, group, stride=layers), :]
            s0[k, rows, :] = (m + change - residual_water) * unit
            sx[k, rows, :] = cx * unit
            sy[k, rows, :] = cy * unit
        return 0

    lax.fori_loop(0, count // group, body, 0)


def saturation_kernel(layers, s0, sx, sy, infil, sig, out):
    count = infil.shape[0]
    group = 32

    def body(step, _):
        rows = pl.ds(pl.multiple_of(step * group, group), group)
        inf = infil[rows, :]
        sg = sig[rows, :]
        for k in range(layers):
            out[pl.ds(step * group * layers + k, group, stride=layers), :] = (
                s0[k, rows, :] + inf * sx[k, rows, :] + sg * sy[k, rows, :]
            )
        return 0

    lax.fori_loop(0, count // group, body, 0)


def unpack_kernel(position, returned, head, land, source, sorted_rows):
    rows, cols = head.shape

    def body(g, _):
        for u in range(32):
            place = position[g * 32 + u]
            sorted_rows[pl.ds(g * 32 + u, 1), :] = returned[pl.ds(place, 1), :]
        return 0

    lax.fori_loop(0, sorted_rows.shape[0] // 32, body, 0)
    for j in range(cols // LANES):
        part = slice(j * LANES, (j + 1) * LANES)
        source[:, part] = (
            store_rate * (head[:, part] * land[:, part].astype(jnp.float32))
            + recharge_gain * sorted_rows[j * rows : (j + 1) * rows, :]
        )


def relax_kernel(
    src, src_r, src_c, mid, mid_r, mid_c, out, t_ref, s_ref, fu, fd, fl, fr, a, b
):
    rows, cols = src.shape
    high, wide = t_ref.shape

    def place(dst, centre, edge, side):
        dst[0:rows, 0:cols] = centre
        dst[rows:high, 0:cols] = edge
        dst[:, cols:wide] = side

    place(s_ref, src[...], src_r[...], src_c[...])
    place(t_ref, mid[0], mid_r[0], mid_c[0])
    place(a, mid[1], mid_r[1], mid_c[1])
    place(b, mid[2], mid_r[2], mid_c[2])
    for g in range(wide // LANES):
        part = slice(g * LANES, (g + 1) * LANES)
        left = slice((g - 1) % (wide // LANES) * LANES, (g - 1) % (wide // LANES) * LANES + LANES)
        right = slice((g + 1) % (wide // LANES) * LANES, (g + 1) % (wide // LANES) * LANES + LANES)
        lane = lax.broadcasted_iota(jnp.int32, (high, LANES), 1)
        t = t_ref[:, part]
        up = 0.5 * (t + pltpu.roll(t, 1, 0))
        down = 0.5 * (t + pltpu.roll(t, high - 1, 0))
        tl = jnp.where(lane == 0, pltpu.roll(t_ref[:, left], 1, 1), pltpu.roll(t, 1, 1))
        tr = jnp.where(
            lane == LANES - 1,
            pltpu.roll(t_ref[:, right], LANES - 1, 1),
            pltpu.roll(t, LANES - 1, 1),
        )
        lf = 0.5 * (t + tl)
        rt = 0.5 * (t + tr)
        inv = b[:, part] / (store_rate + (up + down + lf + rt))
        fu[:, part] = up * inv
        fd[:, part] = down * inv
        fl[:, part] = lf * inv
        fr[:, part] = rt * inv
        s_ref[:, part] = s_ref[:, part] * inv
    now, later = a, b
    for sweep in range(SWEEPS):
        last = sweep == SWEEPS - 1
        for g in range(wide // LANES):
            if last and g * LANES >= cols:
                continue
            part = slice(g * LANES, (g + 1) * LANES)
            lo = (g - 1) % (wide // LANES) * LANES
            hi = (g + 1) % (wide // LANES) * LANES
            lane = lax.broadcasted_iota(jnp.int32, (high, LANES), 1)
            x = now[:, part]
            xl = jnp.where(
                lane == 0, pltpu.roll(now[:, lo : lo + LANES], 1, 1), pltpu.roll(x, 1, 1)
            )
            xr = jnp.where(
                lane == LANES - 1,
                pltpu.roll(now[:, hi : hi + LANES], LANES - 1, 1),
                pltpu.roll(x, LANES - 1, 1),
            )
            y = s_ref[:, part] + fu[:, part] * pltpu.roll(x, 1, 0)
            y = y + fd[:, part] * pltpu.roll(x, high - 1, 0)
            y = y + (fl[:, part] * xl + fr[:, part] * xr)
            if last:
                out[:, part] = y[0:rows]
            else:
                later[:, part] = y
        now, later = later, now


def halos(block):
    rows, cols = block.shape[-2:]

    def shift(x, axis, step):
        count = lax.axis_size(axis)
        if step > 0:
            pairs = [(i, i + 1) for i in range(count - 1)]
        else:
            pairs = [(i + 1, i) for i in range(count - 1)]
        return lax.ppermute(x, axis, pairs)

    above = shift(block[..., rows - SWEEPS :, :], "row", 1)
    below = shift(block[..., :SWEEPS, :], "row", -1)
    edge = jnp.concatenate([below, above], axis=-2)
    first = jnp.concatenate([block[..., :SWEEPS], edge[..., :SWEEPS]], axis=-2)
    final = jnp.concatenate([block[..., cols - SWEEPS :], edge[..., cols - SWEEPS :]], axis=-2)
    right = shift(first, "col", -1)
    left = shift(final, "col", 1)
    gap = jnp.zeros(right.shape[:-1] + (LANES - 2 * SWEEPS,), jnp.float32)
    side = jnp.concatenate([right, gap, left], axis=-1)
    return edge, side


def on_device(precip, head, trans_coef, land, dest, moisture, ksat):
    tile_rows, tile_cols = precip.shape
    peers = lax.axis_size("row") * lax.axis_size("col")
    owned, layers, _ = moisture.shape
    blocks = tile_rows * tile_cols // LANES
    per_peer = (2 * blocks + peers - 1) // peers
    places = peers * per_peer

    target = dest.T.reshape(blocks)
    owner = target // owned
    slot = target - owner * owned
    one_hot = owner[:, None] == jnp.arange(peers, dtype=jnp.int32)[None, :]
    order = jnp.arange(blocks, dtype=jnp.int32)
    earlier = (order[None, :] < order[:, None]).astype(jnp.bfloat16)
    counts = jnp.dot(earlier, one_hot.astype(jnp.bfloat16), preferred_element_type=jnp.float32)
    rank = jnp.sum(jnp.where(one_hot, counts, 0.0), axis=1).astype(jnp.int32)
    position = owner * per_peer + rank
    at_rank = rank[:, None] == jnp.arange(per_peer, dtype=jnp.int32)[None, :]
    values = jnp.concatenate(
        [
            jnp.where(at_rank, order.astype(jnp.float32)[:, None], 0.0),
            jnp.where(at_rank, (slot - owned).astype(jnp.float32)[:, None], 0.0),
        ],
        axis=1,
    )
    table = lax.dot_general(
        one_hot.astype(jnp.float32),
        values,
        (((0,), (0,)), ((), ())),
        precision=lax.Precision.HIGHEST,
        preferred_element_type=jnp.float32,
    )
    slot_source = table[:, :per_peer].astype(jnp.int32).reshape(places)
    labels = jnp.pad(table[:, per_peer:] + float(owned), ((0, 0), (0, LANES - per_peer)))

    depth = 2 * per_peer + 8
    outgoing = pl.pallas_call(
        functools.partial(pack_kernel, peers, per_peer),
        out_shape=f32(peers, depth, LANES),
        in_specs=[SM, VM, VM, VM, VM],
        out_specs=VM,
        scratch_shapes=[pltpu.VMEM((blocks, LANES), jnp.float32)] * 2,
    )(slot_source, labels, precip, head, land)
    arrived = lax.all_to_all(outgoing, ("row", "col"), split_axis=0, concat_axis=0, tiled=True)

    land_share = land.astype(jnp.float32)
    transmit = trans_coef * (1.0 + 0.5 * jnp.tanh(head))
    fixed = jnp.stack([transmit, head * land_share, land_share])
    fixed_r, fixed_c = halos(fixed)

    step = 128
    flat = moisture.reshape(owned * layers, LANES)
    layered = pl.BlockSpec((layers, step, LANES), lambda i: (0, i, 0))
    single = pl.BlockSpec((step, LANES), lambda i: (i, 0))
    natural = pl.BlockSpec((step * layers, LANES), lambda i: (i, 0))
    s0, sx, sy, rec0, rec_x, rec_y = pl.pallas_call(
        functools.partial(factor_kernel, layers, 32),
        grid=(owned // step,),
        out_shape=[f32(layers, owned, LANES)] * 3 + [f32(owned, LANES)] * 3,
        in_specs=[natural, single],
        out_specs=[layered] * 3 + [single] * 3,
        cost_estimate=pl.CostEstimate(
            flops=50 * owned * layers * LANES,
            bytes_accessed=16 * owned * layers * LANES,
            transcendentals=owned * layers * LANES,
        ),
    )(flat, ksat)

    slots = arrived[:, 2 * per_peer, :per_peer].astype(jnp.int32).reshape(places)
    answer, infil, sig = pl.pallas_call(
        functools.partial(owner_kernel, peers, per_peer),
        out_shape=[f32(peers, per_peer, LANES), f32(owned, LANES), f32(owned, LANES)],
        in_specs=[SM, VM, VM, VM, VM],
        out_specs=[VM] * 3,
        scratch_shapes=[pltpu.VMEM((owned + 8, LANES), jnp.float32)] * 3,
    )(slots, arrived, rec0, rec_x, rec_y)
    returned = lax.all_to_all(answer, ("row", "col"), split_axis=0, concat_axis=0, tiled=True)

    saturation = pl.pallas_call(
        functools.partial(saturation_kernel, layers),
        grid=(owned // step,),
        out_shape=f32(owned * layers, LANES),
        in_specs=[layered] * 3 + [single] * 2,
        out_specs=natural,
        cost_estimate=pl.CostEstimate(
            flops=4 * owned * layers * LANES,
            bytes_accessed=16 * owned * layers * LANES,
            transcendentals=0,
        ),
    )(s0, sx, sy, infil, sig).reshape(owned, layers, LANES)

    source = pl.pallas_call(
        unpack_kernel,
        out_shape=f32(tile_rows, tile_cols),
        in_specs=[SM, VM, VM, VM],
        out_specs=VM,
        scratch_shapes=[pltpu.VMEM((blocks, LANES), jnp.float32)],
    )(position, returned.reshape(places, LANES), head, land)
    source_r, source_c = halos(source)

    high, wide = tile_rows + 2 * SWEEPS, tile_cols + LANES
    surface = pl.pallas_call(
        relax_kernel,
        out_shape=f32(tile_rows, tile_cols),
        in_specs=[VM] * 6,
        out_specs=VM,
        scratch_shapes=[pltpu.VMEM((high, wide), jnp.float32)] * 8,
    )(source, source_r, source_c, fixed, fixed_r, fixed_c)
    return (saturation, surface)


def solution(mesh):
    tile = P("row", "col")
    placed = (
        tile,
        tile,
        tile,
        tile,
        tile,
        P(("row", "col"), None, None),
        P(("row", "col"), None),
    )
    return jax.shard_map(
        on_device,
        mesh=mesh,
        in_specs=placed,
        out_specs=(P(("row", "col"), None, None), P("row", "col")),
        check_vma=False,
    )
```

profile of v0, /device:TPU:12, one launch (start us, length us, event | category | flops | bytes accessed | tf_op | source)
XLA Modules:
  0.0 160.5 jit_solution(16946957959947972949)
XLA Ops:
  4.7 5.2 %shard_map.87 = f32[32,136,128]{2,1,0:T(8,128)} custom-call(s32[2048]{0:T(1024)} %reshape.75.src, f32[32,128]{1,0:T(8,128)} %pad.4.labels, f32[256,512]{1,0:T(8,128)} %precip.1, f32[256,512]{1,0:T(8,128)} %head.3, s32[256,512]{1,0:T(8,128)} %land.3), custom_call_target="tpu_custom_call" | custom-call | tf_op jit(solution)/shard_map/pallas_call | solution.py:311
  10.0 6.0 %all-to-all-start = ((f32[32,136,128]{2,1,0:T(8,128)}), f32[32,136,128]{2,1,0:T(8,128)S(1)}, u32[]{:S(2)}, u32[]{:S(2)}) async-start(f32[32,136,128]{2,1,0:T(8,128)} %shard_map.87), calls=%async_computation | async-start | bytes 4456448 | tf_op jit(solution)/shard_map/all_to_all | solution.py:318
  16.0 18.0 %shard_map.86 = (f32[16,1024,128]{2,1,0:T(8,128)}, f32[16,1024,128]{2,1,0:T(8,128)}, f32[16,1024,128]{2,1,0:T(8,128)}, f32[1024,128]{1,0:T(8,128)}, f32[1024,128]{1,0:T(8,128)}, /*index=5*/f32[1024,128]{1,0:T(8,128)}) custom-call(f32[16384,128]{1,0:T(8,128)} %bitcast.12, f32[1024,128]{1,0:T(8,128)} %ksat.1), custom_call_target="tpu_custom_call" | custom-call | flops 104857600 | bytes 33554432 | tf_op jit(solution)/shard_map/pallas_call | solution.py:330
  33.9 31.2 %all-to-all-done.arrived = f32[32,136,128]{2,1,0:T(8,128)S(1)} async-done(((f32[32,136,128]{2,1,0:T(8,128)}), f32[32,136,128]{2,1,0:T(8,128)S(1)}, u32[]{:S(2)}, u32[]{:S(2)}) %all-to-all-start) | async-done | bytes 2228256 | tf_op jit(solution)/shard_map/all_to_all | solution.py:318
  66.5 7.7 %shard_map.88 = (f32[32,64,128]{2,1,0:T(8,128)}, f32[1024,128]{1,0:T(8,128)}, f32[1024,128]{1,0:T(8,128)}) custom-call(s32[2048]{0:T(1024)} %convert_element_type.44.slots, f32[32,136,128]{2,1,0:T(8,128)} %copy-done.1, f32[1024,128]{1,0:T(8,128)} %get-tuple-element.14.rec0, f32[1024,128]{1,0:T(8,128)} %get-tuple-element.15.rec_x, ...), custom_call_target="tpu_custom_call" | custom-call | tf_op jit(solution)/shard_map/pallas_call | solution.py:344
  74.2 6.6 %all-to-all-start.1 = ((f32[32,64,128]{2,1,0:T(8,128)}), f32[32,64,128]{2,1,0:T(8,128)S(1)}, u32[]{:S(2)}, u32[]{:S(2)}) async-start(f32[32,64,128]{2,1,0:T(8,128)} %get-tuple-element.19), calls=%async_computation.1 | async-start | bytes 2097152 | tf_op jit(solution)/shard_map/all_to_all | solution.py:351
  81.3 2.2 %collective-permute-start.4 = (f32[3,4,512]{2,1,0:T(4,128)S(1)}, f32[3,4,512]{2,1,0:T(4,128)S(1)}, u32[]{:S(2)}, u32[]{:S(2)}) collective-permute-start(f32[3,4,512]{2,1,0:T(4,128)S(1)} %get-tuple-element.22), channel_id=1, source_target_pairs={{8,0},{16,8},{24,16},{9,1},{17,9},{25,17},{10,2},{18,10},{26,18},{... | collective-permute-start | bytes 73736 | tf_op jit(solution)/shard_map/ppermute | solution.py:261
  83.4 2.1 %collective-permute-start.5 = (f32[3,4,512]{2,1,0:T(4,128)S(1)}, f32[3,4,512]{2,1,0:T(4,128)S(1)}, u32[]{:S(2)}, u32[]{:S(2)}) collective-permute-start(f32[3,4,512]{2,1,0:T(4,128)S(1)} %get-tuple-element.23), channel_id=1, source_target_pairs={{0,8},{8,16},{16,24},{1,9},{9,17},{17,25},{2,10},{10,18},{18,26},{... | collective-permute-start | bytes 73736 | tf_op jit(solution)/shard_map/ppermute | solution.py:261
  85.9 4.9 %collective-permute-done.5 = f32[3,4,512]{2,1,0:T(4,128)S(1)} collective-permute-done((f32[3,4,512]{2,1,0:T(4,128)S(1)}, f32[3,4,512]{2,1,0:T(4,128)S(1)}, u32[]{:S(2)}, u32[]{:S(2)}) %collective-permute-start.5) | collective-permute-done | bytes 24608 | tf_op jit(solution)/shard_map/ppermute | solution.py:261
  90.9 1.9 %collective-permute-start.6 = (f32[3,264,4]{2,1,0:T(8,128)S(1)}, f32[3,264,4]{2,1,0:T(8,128)S(1)}, u32[]{:S(2)}, u32[]{:S(2)}) collective-permute-start(f32[3,264,4]{2,1,0:T(8,128)S(1)} %pad_maximum_fusion.1), channel_id=1, source_target_pairs={{1,0},{2,1},{3,2},{4,3},{5,4},{6,5},{7,6},{9,8},{10,9},{11,10},{12... | collective-permute-start | bytes 38024 | tf_op jit(solution)/shard_map/ppermute | solution.py:261
  92.9 3.9 %collective-permute-start.7 = (f32[3,264,4]{2,1,0:T(8,128)S(1)}, f32[3,264,4]{2,1,0:T(8,128)S(1)}, u32[]{:S(2)}, u32[]{:S(2)}) collective-permute-start(f32[3,264,4]{2,1,0:T(8,128)S(1)} %pad_maximum_fusion.2), channel_id=1, source_target_pairs={{0,1},{1,2},{2,3},{3,4},{4,5},{5,6},{6,7},{8,9},{9,10},{10,11},{11... | collective-permute-start | bytes 38024 | tf_op jit(solution)/shard_map/ppermute | solution.py:261
  97.5 15.0 %collective-permute-done.6 = f32[3,264,4]{2,1,0:T(8,128)S(1)} collective-permute-done((f32[3,264,4]{2,1,0:T(8,128)S(1)}, f32[3,264,4]{2,1,0:T(8,128)S(1)}, u32[]{:S(2)}, u32[]{:S(2)}) %collective-permute-start.6) | collective-permute-done | bytes 12704 | tf_op jit(solution)/shard_map/ppermute | solution.py:261
  112.4 2.9 %collective-permute-done.7 = f32[3,264,4]{2,1,0:T(8,128)S(1)} collective-permute-done((f32[3,264,4]{2,1,0:T(8,128)S(1)}, f32[3,264,4]{2,1,0:T(8,128)S(1)}, u32[]{:S(2)}, u32[]{:S(2)}) %collective-permute-start.7) | collective-permute-done | bytes 12704 | tf_op jit(solution)/shard_map/ppermute | solution.py:261
  116.3 14.1 %shard_map.89 = f32[16384,128]{1,0:T(8,128)} custom-call(f32[16,1024,128]{2,1,0:T(8,128)} %get-tuple-element.11.s0, f32[16,1024,128]{2,1,0:T(8,128)} %get-tuple-element.12.sx, f32[16,1024,128]{2,1,0:T(8,128)} %get-tuple-element.13.sy, f32[1024,128]{1,0:T(8,128)} %get-tuple-element.17.infil, f32[1024,128]{1,0:T(8,128)} %get-tuple-element.18.sig), custom_call_target="tpu_custom_call" | custom-call | flops 8388608 | bytes 33554432 | tf_op jit(solution)/shard_map/pallas_call | solution.py:353
  131.4 3.4 %shard_map.90.src = f32[256,512]{1,0:T(8,128)} custom-call(s32[1024]{0:T(1024)} %get-tuple-element.36.position, f32[2048,128]{1,0:T(8,128)} %bitcast.14, f32[256,512]{1,0:T(8,128)} %head.3, s32[256,512]{1,0:T(8,128)} %land.3), custom_call_target="tpu_custom_call" | custom-call | tf_op jit(solution)/shard_map/pallas_call | solution.py:366
  135.5 3.0 %collective-permute-start = (f32[4,512]{1,0:T(4,128)S(1)}, f32[4,512]{1,0:T(4,128)S(1)}, u32[]{:S(2)}, u32[]{:S(2)}) collective-permute-start(f32[4,512]{1,0:T(4,128)S(1)} %get-tuple-element.28), channel_id=1, source_target_pairs={{8,0},{16,8},{24,16},{9,1},{17,9},{25,17},{10,2},{18,10},{26,18},{... | collective-permute-start | bytes 24584 | tf_op jit(solution)/shard_map/ppermute | solution.py:261
  138.5 1.9 %collective-permute-start.1 = (f32[4,512]{1,0:T(4,128)S(1)}, f32[4,512]{1,0:T(4,128)S(1)}, u32[]{:S(2)}, u32[]{:S(2)}) collective-permute-start(f32[4,512]{1,0:T(4,128)S(1)} %get-tuple-element.29), channel_id=1, source_target_pairs={{0,8},{8,16},{16,24},{1,9},{9,17},{17,25},{2,10},{10,18},{18,26},{... | collective-permute-start | bytes 24584 | tf_op jit(solution)/shard_map/ppermute | solution.py:261
  140.4 1.1 fusion.21
  141.5 2.0 %collective-permute-done.1 = f32[4,512]{1,0:T(4,128)S(1)} collective-permute-done((f32[4,512]{1,0:T(4,128)S(1)}, f32[4,512]{1,0:T(4,128)S(1)}, u32[]{:S(2)}, u32[]{:S(2)}) %collective-permute-start.1) | collective-permute-done | bytes 8224 | tf_op jit(solution)/shard_map/ppermute | solution.py:261
  143.6 1.9 %collective-permute-start.2 = (f32[264,4]{1,0:T(8,128)S(1)}, f32[264,4]{1,0:T(8,128)S(1)}, u32[]{:S(2)}, u32[]{:S(2)}) collective-permute-start(f32[264,4]{1,0:T(8,128)S(1)} %pad_maximum_fusion.4), channel_id=1, source_target_pairs={{1,0},{2,1},{3,2},{4,3},{5,4},{6,5},{7,6},{9,8},{10,9},{11,10},{12... | collective-permute-start | bytes 12680 | tf_op jit(solution)/shard_map/ppermute | solution.py:261
  145.5 4.1 %collective-permute-start.3 = (f32[264,4]{1,0:T(8,128)S(1)}, f32[264,4]{1,0:T(8,128)S(1)}, u32[]{:S(2)}, u32[]{:S(2)}) collective-permute-start(f32[264,4]{1,0:T(8,128)S(1)} %pad_maximum_fusion.5), channel_id=1, source_target_pairs={{0,1},{1,2},{2,3},{3,4},{4,5},{5,6},{6,7},{8,9},{9,10},{10,11},{11... | collective-permute-start | bytes 12680 | tf_op jit(solution)/shard_map/ppermute | solution.py:261
  150.2 1.7 %collective-permute-done.2 = f32[264,4]{1,0:T(8,128)S(1)} collective-permute-done((f32[264,4]{1,0:T(8,128)S(1)}, f32[264,4]{1,0:T(8,128)S(1)}, u32[]{:S(2)}, u32[]{:S(2)}) %collective-permute-start.2) | collective-permute-done | bytes 4256 | tf_op jit(solution)/shard_map/ppermute | solution.py:261
  151.9 1.4 collective-permute-done.3
  154.1 6.4 %shard_map.91 = f32[256,512]{1,0:T(8,128)} custom-call(f32[256,512]{1,0:T(8,128)} %shard_map.90.src, f32[8,512]{1,0:T(8,128)} %pad_maximum_fusion.8.src_r, f32[264,128]{1,0:T(8,128)} %pad_maximum_fusion.6.src_c, f32[3,256,512]{2,1,0:T(8,128)} %copy-done, f32[3,8,512]{2,1,0:T(8,128)} %pad_maximum_fusion.7.mid_r, f32[3,264,128]{2,1,0:T(8,128)} %pad_maximum_fusion.3.mid_c), custom_call_target="tpu_custom_call" | custom-call | tf_op jit(solution)/shard_map/pallas_call | solution.py:376
  (45 shorter events, 11.0 us)
Async XLA Ops:
  10.0 55.1 %all-to-all-start = ((f32[32,136,128]{2,1,0:T(8,128)}), f32[32,136,128]{2,1,0:T(8,128)S(1)}, u32[]{:S(2)}, u32[]{:S(2)}) async-start(f32[32,136,128]{2,1,0:T(8,128)} %shard_map.87), calls=%async_computation | async-start | bytes 4456448 | tf_op jit(solution)/shard_map/all_to_all | solution.py:318
  65.1 1.4 copy-start.1
  66.5 14.4 %copy-start.2 = (s32[256,512]{1,0:T(8,128)S(1)}, s32[256,512]{1,0:T(8,128)}, u32[]{:S(2)}) copy-start(s32[256,512]{1,0:T(8,128)} %land.3) | copy-start | bytes 1572868
  74.2 6.7 %copy-start.3 = (f32[256,512]{1,0:T(8,128)S(1)}, f32[256,512]{1,0:T(8,128)}, u32[]{:S(2)}) copy-start(f32[256,512]{1,0:T(8,128)} %head.3) | copy-start | bytes 1572868
  74.2 6.7 %copy-start.5 = (f32[256,512]{1,0:T(8,128)S(1)}, f32[256,512]{1,0:T(8,128)}, u32[]{:S(2)}) copy-start(f32[256,512]{1,0:T(8,128)} %param.9) | copy-start | bytes 1572868
  74.2 56.2 %all-to-all-start.1 = ((f32[32,64,128]{2,1,0:T(8,128)}), f32[32,64,128]{2,1,0:T(8,128)S(1)}, u32[]{:S(2)}, u32[]{:S(2)}) async-start(f32[32,64,128]{2,1,0:T(8,128)} %get-tuple-element.19), calls=%async_computation.1 | async-start | bytes 2097152 | tf_op jit(solution)/shard_map/all_to_all | solution.py:351
  81.2 35.1 %copy-start = (f32[3,256,512]{2,1,0:T(8,128)}, f32[3,256,512]{2,1,0:T(8,128)S(1)}, u32[]{:S(2)}) copy-start(f32[3,256,512]{2,1,0:T(8,128)S(1)} %pad_maximum_fusion.mid) | copy-start | bytes 4718596
  81.3 4.6 %collective-permute-start.4 = (f32[3,4,512]{2,1,0:T(4,128)S(1)}, f32[3,4,512]{2,1,0:T(4,128)S(1)}, u32[]{:S(2)}, u32[]{:S(2)}) collective-permute-start(f32[3,4,512]{2,1,0:T(4,128)S(1)} %get-tuple-element.22), channel_id=1, source_target_pairs={{8,0},{16,8},{24,16},{9,1},{17,9},{25,17},{10,2},{18,10},{26,18},{... | collective-permute-start | bytes 73736 | tf_op jit(solution)/shard_map/ppermute | solution.py:261
  83.4 7.4 %collective-permute-start.5 = (f32[3,4,512]{2,1,0:T(4,128)S(1)}, f32[3,4,512]{2,1,0:T(4,128)S(1)}, u32[]{:S(2)}, u32[]{:S(2)}) collective-permute-start(f32[3,4,512]{2,1,0:T(4,128)S(1)} %get-tuple-element.23), channel_id=1, source_target_pairs={{0,8},{8,16},{16,24},{1,9},{9,17},{17,25},{2,10},{10,18},{18,26},{... | collective-permute-start | bytes 73736 | tf_op jit(solution)/shard_map/ppermute | solution.py:261
  90.9 21.5 %collective-permute-start.6 = (f32[3,264,4]{2,1,0:T(8,128)S(1)}, f32[3,264,4]{2,1,0:T(8,128)S(1)}, u32[]{:S(2)}, u32[]{:S(2)}) collective-permute-start(f32[3,264,4]{2,1,0:T(8,128)S(1)} %pad_maximum_fusion.1), channel_id=1, source_target_pairs={{1,0},{2,1},{3,2},{4,3},{5,4},{6,5},{7,6},{9,8},{10,9},{11,10},{12... | collective-permute-start | bytes 38024 | tf_op jit(solution)/shard_map/ppermute | solution.py:261
  92.9 22.4 %collective-permute-start.7 = (f32[3,264,4]{2,1,0:T(8,128)S(1)}, f32[3,264,4]{2,1,0:T(8,128)S(1)}, u32[]{:S(2)}, u32[]{:S(2)}) collective-permute-start(f32[3,264,4]{2,1,0:T(8,128)S(1)} %pad_maximum_fusion.2), channel_id=1, source_target_pairs={{0,1},{1,2},{2,3},{3,4},{4,5},{5,6},{6,7},{8,9},{9,10},{10,11},{11... | collective-permute-start | bytes 38024 | tf_op jit(solution)/shard_map/ppermute | solution.py:261
  130.4 1.0 copy-start.4
  135.5 6.0 %collective-permute-start = (f32[4,512]{1,0:T(4,128)S(1)}, f32[4,512]{1,0:T(4,128)S(1)}, u32[]{:S(2)}, u32[]{:S(2)}) collective-permute-start(f32[4,512]{1,0:T(4,128)S(1)} %get-tuple-element.28), channel_id=1, source_target_pairs={{8,0},{16,8},{24,16},{9,1},{17,9},{25,17},{10,2},{18,10},{26,18},{... | collective-permute-start | bytes 24584 | tf_op jit(solution)/shard_map/ppermute | solution.py:261
  138.5 5.0 %collective-permute-start.1 = (f32[4,512]{1,0:T(4,128)S(1)}, f32[4,512]{1,0:T(4,128)S(1)}, u32[]{:S(2)}, u32[]{:S(2)}) collective-permute-start(f32[4,512]{1,0:T(4,128)S(1)} %get-tuple-element.29), channel_id=1, source_target_pairs={{0,8},{8,16},{16,24},{1,9},{9,17},{17,25},{2,10},{10,18},{18,26},{... | collective-permute-start | bytes 24584 | tf_op jit(solution)/shard_map/ppermute | solution.py:261
  143.6 8.4 %collective-permute-start.2 = (f32[264,4]{1,0:T(8,128)S(1)}, f32[264,4]{1,0:T(8,128)S(1)}, u32[]{:S(2)}, u32[]{:S(2)}) collective-permute-start(f32[264,4]{1,0:T(8,128)S(1)} %pad_maximum_fusion.4), channel_id=1, source_target_pairs={{1,0},{2,1},{3,2},{4,3},{5,4},{6,5},{7,6},{9,8},{10,9},{11,10},{12... | collective-permute-start | bytes 12680 | tf_op jit(solution)/shard_map/ppermute | solution.py:261
  145.5 7.8 %collective-permute-start.3 = (f32[264,4]{1,0:T(8,128)S(1)}, f32[264,4]{1,0:T(8,128)S(1)}, u32[]{:S(2)}, u32[]{:S(2)}) collective-permute-start(f32[264,4]{1,0:T(8,128)S(1)} %pad_maximum_fusion.5), channel_id=1, source_target_pairs={{0,1},{1,2},{2,3},{3,4},{4,5},{5,6},{6,7},{8,9},{9,10},{10,11},{11... | collective-permute-start | bytes 12680 | tf_op jit(solution)/shard_map/ppermute | solution.py:261
where the time goes:
time: 163 us; the launch traced here: 160 us
  waiting for transfers between devices  59.1 us (36%)
  Pallas kernels  54.8 us (34%)
  starting transfers between devices  33.7 us (21%)
  local copies, waits for them, and re-layouts  6.35 us (4%)
  other arithmetic  4.72 us (3%)
    all_to_all x1, waiting for transfers between devices, on_device(): lax.all_to_all(outgoing, ('row', 'col'), split_axis=0, concat_axis=0, til...  31.2 us
    ppermute x8, waiting for transfers between devices, shift(): return lax.ppermute(x, axis, pairs)  27.9 us
    ppermute x8, starting transfers between devices, shift(): return lax.ppermute(x, axis, pairs)  21.1 us
    pallas_call x1, Pallas kernels, on_device(): pl.pallas_call(functools.partial(factor_kernel, layers, 32), grid=(owned...  18 us
    pallas_call x1, Pallas kernels, on_device(): pl.pallas_call(functools.partial(saturation_kernel, layers), grid=(owned...  14.1 us
    pallas_call x1, Pallas kernels, on_device(): pl.pallas_call(functools.partial(owner_kernel, peers, per_peer), out_shap...  7.72 us
    all_to_all x1, starting transfers between devices, on_device(): lax.all_to_all(answer, ('row', 'col'), split_axis=0, concat_axis=0, tiled...  6.62 us
    pallas_call x1, Pallas kernels, on_device(): pl.pallas_call(relax_kernel, out_shape=f32(tile_rows, tile_cols), in_spec...  6.39 us
  transfers between devices with their start and end apart: 10, of which 7 were waited for; matrix products, arithmetic and copies ran while one was open for 2% of the time, Pallas kernels for 20%

commit v1 on v0

--- a/solution.py
+++ b/solution.py
@@ -340,6 +340,7 @@
         ),
     )(flat, ksat)
 
+    arrived, fixed_r, fixed_c = lax.optimization_barrier((arrived, fixed_r, fixed_c))
     slots = arrived[:, 2 * per_peer, :per_peer].astype(jnp.int32).reshape(places)
     answer, infil, sig = pl.pallas_call(
         functools.partial(owner_kernel, peers, per_peer),

time: 163 us -> 148 us (0.908); the launches traced: 160 us -> 147 us
  waiting for transfers between devices: 59.1 us -> 39.6 us
  starting transfers between devices: 33.7 us -> 39.6 us
    all_to_all x1, waiting for transfers between devices: 31.2 us -> 0.01 us  [on_device(): lax.all_to_all(outgoing, ('row', 'col'), split_axis=0, concat_axis=0, til...]
    all_to_all x1, waiting for transfers between devices: 0.01 us -> 10.9 us  [on_device(): lax.all_to_all(answer, ('row', 'col'), split_axis=0, concat_axis=0, tiled...]
    all_to_all x1, starting transfers between devices: 6.62 us -> 12.3 us  [on_device(): lax.all_to_all(answer, ('row', 'col'), split_axis=0, concat_axis=0, tiled...]
  transfers between devices with their start and end apart: 10 -> 10, of which waited for: 7 -> 6; matrix products, arithmetic and copies ran while one was open for 2% -> 3% of each run, Pallas kernels for 20% -> 22%
where the time goes in v1:
time: 148 us; the launch traced here: 147 us
  Pallas kernels  54.9 us (37%)
  starting transfers between devices  39.6 us (27%)
  waiting for transfers between devices  39.6 us (27%)
  local copies, waits for them, and re-layouts  5.73 us (4%)
  other arithmetic  5.66 us (4%)
    ppermute x8, waiting for transfers between devices, shift(): return lax.ppermute(x, axis, pairs)  28.7 us
    ppermute x8, starting transfers between devices, shift(): return lax.ppermute(x, axis, pairs)  21.2 us
    pallas_call x1, Pallas kernels, on_device(): pl.pallas_call(functools.partial(factor_kernel, layers, 32), grid=(owned...  18 us
    pallas_call x1, Pallas kernels, on_device(): pl.pallas_call(functools.partial(saturation_kernel, layers), grid=(owned...  14.1 us
    all_to_all x1, starting transfers between devices, on_device(): lax.all_to_all(answer, ('row', 'col'), split_axis=0, concat_axis=0, tiled...  12.3 us
    all_to_all x1, waiting for transfers between devices, on_device(): lax.all_to_all(answer, ('row', 'col'), split_axis=0, concat_axis=0, tiled...  10.9 us
    pallas_call x1, Pallas kernels, on_device(): pl.pallas_call(functools.partial(owner_kernel, peers, per_peer), out_shap...  7.77 us
    pallas_call x1, Pallas kernels, on_device(): pl.pallas_call(relax_kernel, out_shape=f32(tile_rows, tile_cols), in_spec...  6.39 us
  transfers between devices with their start and end apart: 10, of which 6 were waited for; matrix products, arithmetic and copies ran while one was open for 3% of the time, Pallas kernels for 22%

profile of v1, /device:TPU:12, one launch (start us, length us, event | category | flops | bytes accessed | tf_op | source)
XLA Modules:
  0.0 147.3 jit_solution(12204205610017621788)
XLA Ops:
  4.7 5.2 %shard_map.87 = f32[32,136,128]{2,1,0:T(8,128)} custom-call(s32[2048]{0:T(1024)} %reshape.75.src, f32[32,128]{1,0:T(8,128)} %pad.4.labels, f32[256,512]{1,0:T(8,128)} %precip.1, f32[256,512]{1,0:T(8,128)} %head.3, s32[256,512]{1,0:T(8,128)} %land.3), custom_call_target="tpu_custom_call" | custom-call | tf_op jit(solution)/shard_map/pallas_call | solution.py:311
  10.0 6.0 %all-to-all-start = ((f32[32,136,128]{2,1,0:T(8,128)}), f32[32,136,128]{2,1,0:T(8,128)}, u32[]{:S(2)}, u32[]{:S(2)}) async-start(f32[32,136,128]{2,1,0:T(8,128)} %shard_map.87), calls=%async_computation | async-start | bytes 4456448 | tf_op jit(solution)/shard_map/all_to_all | solution.py:318
  16.5 2.2 %collective-permute-start = (f32[3,4,512]{2,1,0:T(4,128)S(1)}, f32[3,4,512]{2,1,0:T(4,128)S(1)}, u32[]{:S(2)}, u32[]{:S(2)}) collective-permute-start(f32[3,4,512]{2,1,0:T(4,128)S(1)} %get-tuple-element.28), channel_id=1, source_target_pairs={{8,0},{16,8},{24,16},{9,1},{17,9},{25,17},{10,2},{18,10},{26,18},{... | collective-permute-start | bytes 73736 | tf_op jit(solution)/shard_map/ppermute | solution.py:261
  18.7 2.1 %collective-permute-start.1 = (f32[3,4,512]{2,1,0:T(4,128)S(1)}, f32[3,4,512]{2,1,0:T(4,128)S(1)}, u32[]{:S(2)}, u32[]{:S(2)}) collective-permute-start(f32[3,4,512]{2,1,0:T(4,128)S(1)} %get-tuple-element.29), channel_id=1, source_target_pairs={{0,8},{8,16},{16,24},{1,9},{9,17},{17,25},{2,10},{10,18},{18,26},{... | collective-permute-start | bytes 73736 | tf_op jit(solution)/shard_map/ppermute | solution.py:261
  21.1 18.0 %shard_map.86 = (f32[16,1024,128]{2,1,0:T(8,128)}, f32[16,1024,128]{2,1,0:T(8,128)}, f32[16,1024,128]{2,1,0:T(8,128)}, f32[1024,128]{1,0:T(8,128)}, f32[1024,128]{1,0:T(8,128)}, /*index=5*/f32[1024,128]{1,0:T(8,128)}) custom-call(f32[16384,128]{1,0:T(8,128)} %bitcast.12, f32[1024,128]{1,0:T(8,128)} %ksat.1), custom_call_target="tpu_custom_call" | custom-call | flops 104857600 | bytes 33554432 | tf_op jit(solution)/shard_map/pallas_call | solution.py:330
  39.2 3.4 %collective-permute-start.2 = (f32[3,264,4]{2,1,0:T(8,128)S(1)}, f32[3,264,4]{2,1,0:T(8,128)S(1)}, u32[]{:S(2)}, u32[]{:S(2)}) collective-permute-start(f32[3,264,4]{2,1,0:T(8,128)S(1)} %pad_maximum_fusion.1), channel_id=1, source_target_pairs={{1,0},{2,1},{3,2},{4,3},{5,4},{6,5},{7,6},{9,8},{10,9},{11,10},{12... | collective-permute-start | bytes 38024 | tf_op jit(solution)/shard_map/ppermute | solution.py:261
  42.6 2.5 %collective-permute-start.3 = (f32[3,264,4]{2,1,0:T(8,128)S(1)}, f32[3,264,4]{2,1,0:T(8,128)S(1)}, u32[]{:S(2)}, u32[]{:S(2)}) collective-permute-start(f32[3,264,4]{2,1,0:T(8,128)S(1)} %pad_maximum_fusion.2), channel_id=1, source_target_pairs={{0,1},{1,2},{2,3},{3,4},{4,5},{5,6},{6,7},{8,9},{9,10},{10,11},{11... | collective-permute-start | bytes 38024 | tf_op jit(solution)/shard_map/ppermute | solution.py:261
  45.7 13.7 %collective-permute-done.2 = f32[3,264,4]{2,1,0:T(8,128)S(1)} collective-permute-done((f32[3,264,4]{2,1,0:T(8,128)S(1)}, f32[3,264,4]{2,1,0:T(8,128)S(1)}, u32[]{:S(2)}, u32[]{:S(2)}) %collective-permute-start.2) | collective-permute-done | bytes 12704 | tf_op jit(solution)/shard_map/ppermute | solution.py:261
  59.4 8.0 %collective-permute-done.3 = f32[3,264,4]{2,1,0:T(8,128)S(1)} collective-permute-done((f32[3,264,4]{2,1,0:T(8,128)S(1)}, f32[3,264,4]{2,1,0:T(8,128)S(1)}, u32[]{:S(2)}, u32[]{:S(2)}) %collective-permute-start.3) | collective-permute-done | bytes 12704 | tf_op jit(solution)/shard_map/ppermute | solution.py:261
  67.3 1.0 pad_maximum_fusion.3.mid_c
  69.9 7.8 %shard_map.88 = (f32[32,64,128]{2,1,0:T(8,128)}, f32[1024,128]{1,0:T(8,128)}, f32[1024,128]{1,0:T(8,128)}) custom-call(s32[2048]{0:T(1024)} %convert_element_type.45.slots, f32[32,136,128]{2,1,0:T(8,128)} %all-to-all-done.arrived, f32[1024,128]{1,0:T(8,128)} %get-tuple-element.18.rec0, f32[1024,128]{1,0:T(8,128)} %get-tuple-element.19.rec_x, ...), custom_call_target="tpu_custom_call" | custom-call | tf_op jit(solution)/shard_map/pallas_call | solution.py:345
  77.7 12.3 %all-to-all-start.1 = ((f32[32,64,128]{2,1,0:T(8,128)}), f32[32,64,128]{2,1,0:T(8,128)S(1)}, u32[]{:S(2)}, u32[]{:S(2)}) async-start(f32[32,64,128]{2,1,0:T(8,128)} %get-tuple-element.23), calls=%async_computation.1 | async-start | bytes 2097152 | tf_op jit(solution)/shard_map/all_to_all | solution.py:352
  90.0 14.1 %shard_map.89 = f32[16384,128]{1,0:T(8,128)} custom-call(f32[16,1024,128]{2,1,0:T(8,128)} %get-tuple-element.14.s0, f32[16,1024,128]{2,1,0:T(8,128)} %get-tuple-element.15.sx, f32[16,1024,128]{2,1,0:T(8,128)} %get-tuple-element.16.sy, f32[1024,128]{1,0:T(8,128)} %get-tuple-element.21.infil, f32[1024,128]{1,0:T(8,128)} %get-tuple-element.22.sig), custom_call_target="tpu_custom_call" | custom-call | flops 8388608 | bytes 33554432 | tf_op jit(solution)/shard_map/pallas_call | solution.py:354
  104.1 10.9 %all-to-all-done.1 = f32[32,64,128]{2,1,0:T(8,128)S(1)} async-done(((f32[32,64,128]{2,1,0:T(8,128)}), f32[32,64,128]{2,1,0:T(8,128)S(1)}, u32[]{:S(2)}, u32[]{:S(2)}) %all-to-all-start.1) | async-done | bytes 1048608 | tf_op jit(solution)/shard_map/all_to_all | solution.py:352
  115.1 1.0 copy-done.3
  116.1 3.4 %shard_map.90.src = f32[256,512]{1,0:T(8,128)} custom-call(s32[1024]{0:T(1024)} %get-tuple-element.42.position, f32[2048,128]{1,0:T(8,128)} %bitcast.14, f32[256,512]{1,0:T(8,128)} %head.3, s32[256,512]{1,0:T(8,128)} %land.3), custom_call_target="tpu_custom_call" | custom-call | tf_op jit(solution)/shard_map/pallas_call | solution.py:367
  120.2 3.3 %collective-permute-start.4 = (f32[4,512]{1,0:T(4,128)S(1)}, f32[4,512]{1,0:T(4,128)S(1)}, u32[]{:S(2)}, u32[]{:S(2)}) collective-permute-start(f32[4,512]{1,0:T(4,128)S(1)} %get-tuple-element.32), channel_id=1, source_target_pairs={{8,0},{16,8},{24,16},{9,1},{17,9},{25,17},{10,2},{18,10},{26,18},{... | collective-permute-start | bytes 24584 | tf_op jit(solution)/shard_map/ppermute | solution.py:261
  123.5 1.9 %collective-permute-start.5 = (f32[4,512]{1,0:T(4,128)S(1)}, f32[4,512]{1,0:T(4,128)S(1)}, u32[]{:S(2)}, u32[]{:S(2)}) collective-permute-start(f32[4,512]{1,0:T(4,128)S(1)} %get-tuple-element.33), channel_id=1, source_target_pairs={{0,8},{8,16},{16,24},{1,9},{9,17},{17,25},{2,10},{10,18},{18,26},{... | collective-permute-start | bytes 24584 | tf_op jit(solution)/shard_map/ppermute | solution.py:261
  125.5 1.1 fusion.20
  126.5 2.0 %collective-permute-done.5 = f32[4,512]{1,0:T(4,128)S(1)} collective-permute-done((f32[4,512]{1,0:T(4,128)S(1)}, f32[4,512]{1,0:T(4,128)S(1)}, u32[]{:S(2)}, u32[]{:S(2)}) %collective-permute-start.5) | collective-permute-done | bytes 8224 | tf_op jit(solution)/shard_map/ppermute | solution.py:261
  128.6 3.7 %collective-permute-start.6 = (f32[264,4]{1,0:T(8,128)S(1)}, f32[264,4]{1,0:T(8,128)S(1)}, u32[]{:S(2)}, u32[]{:S(2)}) collective-permute-start(f32[264,4]{1,0:T(8,128)S(1)} %pad_maximum_fusion.4), channel_id=1, source_target_pairs={{1,0},{2,1},{3,2},{4,3},{5,4},{6,5},{7,6},{9,8},{10,9},{11,10},{12... | collective-permute-start | bytes 12680 | tf_op jit(solution)/shard_map/ppermute | solution.py:261
  132.3 2.1 %collective-permute-start.7 = (f32[264,4]{1,0:T(8,128)S(1)}, f32[264,4]{1,0:T(8,128)S(1)}, u32[]{:S(2)}, u32[]{:S(2)}) collective-permute-start(f32[264,4]{1,0:T(8,128)S(1)} %pad_maximum_fusion.5), channel_id=1, source_target_pairs={{0,1},{1,2},{2,3},{3,4},{4,5},{5,6},{6,7},{8,9},{9,10},{10,11},{11... | collective-permute-start | bytes 12680 | tf_op jit(solution)/shard_map/ppermute | solution.py:261
  135.5 4.6 %collective-permute-done.7 = f32[264,4]{1,0:T(8,128)S(1)} collective-permute-done((f32[264,4]{1,0:T(8,128)S(1)}, f32[264,4]{1,0:T(8,128)S(1)}, u32[]{:S(2)}, u32[]{:S(2)}) %collective-permute-start.7) | collective-permute-done | bytes 4256 | tf_op jit(solution)/shard_map/ppermute | solution.py:261
  140.9 6.4 %shard_map.91 = f32[256,512]{1,0:T(8,128)} custom-call(f32[256,512]{1,0:T(8,128)} %shard_map.90.src, f32[8,512]{1,0:T(8,128)} %pad_maximum_fusion.8.src_r, f32[264,128]{1,0:T(8,128)} %pad_maximum_fusion.6.src_c, f32[3,256,512]{2,1,0:T(8,128)} %copy-done, f32[3,8,512]{2,1,0:T(8,128)} %pad_maximum_fusion.7.mid_r, f32[3,264,128]{2,1,0:T(8,128)} %pad_maximum_fusion.3.mid_c), custom_call_target="tpu_custom_call" | custom-call | tf_op jit(solution)/shard_map/pallas_call | solution.py:377
  (43 shorter events, 9.7 us)
Async XLA Ops:
  10.0 6.1 %copy-start.1 = (s32[256,512]{1,0:T(8,128)S(1)}, s32[256,512]{1,0:T(8,128)}, u32[]{:S(2)}) copy-start(s32[256,512]{1,0:T(8,128)} %land.3) | copy-start | bytes 1572868
  10.0 6.1 %copy-start.2 = (f32[256,512]{1,0:T(8,128)S(1)}, f32[256,512]{1,0:T(8,128)}, u32[]{:S(2)}) copy-start(f32[256,512]{1,0:T(8,128)} %head.3) | copy-start | bytes 1572868
  10.0 6.1 %copy-start.4 = (f32[256,512]{1,0:T(8,128)S(1)}, f32[256,512]{1,0:T(8,128)}, u32[]{:S(2)}) copy-start(f32[256,512]{1,0:T(8,128)} %param.9) | copy-start | bytes 1572868
  10.0 58.3 %all-to-all-start = ((f32[32,136,128]{2,1,0:T(8,128)}), f32[32,136,128]{2,1,0:T(8,128)}, u32[]{:S(2)}, u32[]{:S(2)}) async-start(f32[32,136,128]{2,1,0:T(8,128)} %shard_map.87), calls=%async_computation | async-start | bytes 4456448 | tf_op jit(solution)/shard_map/all_to_all | solution.py:318
  16.4 22.6 %copy-start = (f32[3,256,512]{2,1,0:T(8,128)}, f32[3,256,512]{2,1,0:T(8,128)S(1)}, u32[]{:S(2)}) copy-start(f32[3,256,512]{2,1,0:T(8,128)S(1)} %pad_maximum_fusion.mid) | copy-start | bytes 4718596
  16.5 22.6 %collective-permute-start = (f32[3,4,512]{2,1,0:T(4,128)S(1)}, f32[3,4,512]{2,1,0:T(4,128)S(1)}, u32[]{:S(2)}, u32[]{:S(2)}) collective-permute-start(f32[3,4,512]{2,1,0:T(4,128)S(1)} %get-tuple-element.28), channel_id=1, source_target_pairs={{8,0},{16,8},{24,16},{9,1},{17,9},{25,17},{10,2},{18,10},{26,18},{... | collective-permute-start | bytes 73736 | tf_op jit(solution)/shard_map/ppermute | solution.py:261
  18.7 20.4 %collective-permute-start.1 = (f32[3,4,512]{2,1,0:T(4,128)S(1)}, f32[3,4,512]{2,1,0:T(4,128)S(1)}, u32[]{:S(2)}, u32[]{:S(2)}) collective-permute-start(f32[3,4,512]{2,1,0:T(4,128)S(1)} %get-tuple-element.29), channel_id=1, source_target_pairs={{0,8},{8,16},{16,24},{1,9},{9,17},{17,25},{2,10},{10,18},{18,26},{... | collective-permute-start | bytes 73736 | tf_op jit(solution)/shard_map/ppermute | solution.py:261
  39.2 20.2 %collective-permute-start.2 = (f32[3,264,4]{2,1,0:T(8,128)S(1)}, f32[3,264,4]{2,1,0:T(8,128)S(1)}, u32[]{:S(2)}, u32[]{:S(2)}) collective-permute-start(f32[3,264,4]{2,1,0:T(8,128)S(1)} %pad_maximum_fusion.1), channel_id=1, source_target_pairs={{1,0},{2,1},{3,2},{4,3},{5,4},{6,5},{7,6},{9,8},{10,9},{11,10},{12... | collective-permute-start | bytes 38024 | tf_op jit(solution)/shard_map/ppermute | solution.py:261
  42.6 24.8 %collective-permute-start.3 = (f32[3,264,4]{2,1,0:T(8,128)S(1)}, f32[3,264,4]{2,1,0:T(8,128)S(1)}, u32[]{:S(2)}, u32[]{:S(2)}) collective-permute-start(f32[3,264,4]{2,1,0:T(8,128)S(1)} %pad_maximum_fusion.2), channel_id=1, source_target_pairs={{0,1},{1,2},{2,3},{3,4},{4,5},{5,6},{6,7},{8,9},{9,10},{10,11},{11... | collective-permute-start | bytes 38024 | tf_op jit(solution)/shard_map/ppermute | solution.py:261
  77.7 37.4 %all-to-all-start.1 = ((f32[32,64,128]{2,1,0:T(8,128)}), f32[32,64,128]{2,1,0:T(8,128)S(1)}, u32[]{:S(2)}, u32[]{:S(2)}) async-start(f32[32,64,128]{2,1,0:T(8,128)} %get-tuple-element.23), calls=%async_computation.1 | async-start | bytes 2097152 | tf_op jit(solution)/shard_map/all_to_all | solution.py:352
  115.1 1.0 copy-start.3
  120.2 6.3 %collective-permute-start.4 = (f32[4,512]{1,0:T(4,128)S(1)}, f32[4,512]{1,0:T(4,128)S(1)}, u32[]{:S(2)}, u32[]{:S(2)}) collective-permute-start(f32[4,512]{1,0:T(4,128)S(1)} %get-tuple-element.32), channel_id=1, source_target_pairs={{8,0},{16,8},{24,16},{9,1},{17,9},{25,17},{10,2},{18,10},{26,18},{... | collective-permute-start | bytes 24584 | tf_op jit(solution)/shard_map/ppermute | solution.py:261
  123.5 5.0 %collective-permute-start.5 = (f32[4,512]{1,0:T(4,128)S(1)}, f32[4,512]{1,0:T(4,128)S(1)}, u32[]{:S(2)}, u32[]{:S(2)}) collective-permute-start(f32[4,512]{1,0:T(4,128)S(1)} %get-tuple-element.33), channel_id=1, source_target_pairs={{0,8},{8,16},{16,24},{1,9},{9,17},{17,25},{2,10},{10,18},{18,26},{... | collective-permute-start | bytes 24584 | tf_op jit(solution)/shard_map/ppermute | solution.py:261
  128.6 6.9 %collective-permute-start.6 = (f32[264,4]{1,0:T(8,128)S(1)}, f32[264,4]{1,0:T(8,128)S(1)}, u32[]{:S(2)}, u32[]{:S(2)}) collective-permute-start(f32[264,4]{1,0:T(8,128)S(1)} %pad_maximum_fusion.4), channel_id=1, source_target_pairs={{1,0},{2,1},{3,2},{4,3},{5,4},{6,5},{7,6},{9,8},{10,9},{11,10},{12... | collective-permute-start | bytes 12680 | tf_op jit(solution)/shard_map/ppermute | solution.py:261
  132.3 7.8 %collective-permute-start.7 = (f32[264,4]{1,0:T(8,128)S(1)}, f32[264,4]{1,0:T(8,128)S(1)}, u32[]{:S(2)}, u32[]{:S(2)}) collective-permute-start(f32[264,4]{1,0:T(8,128)S(1)} %pad_maximum_fusion.5), channel_id=1, source_target_pairs={{0,1},{1,2},{2,3},{3,4},{4,5},{5,6},{6,7},{8,9},{9,10},{10,11},{11... | collective-permute-start | bytes 12680 | tf_op jit(solution)/shard_map/ppermute | solution.py:261

commit v2 on v1

--- a/solution.py
+++ b/solution.py
@@ -265,8 +265,8 @@
     edge = jnp.concatenate([below, above], axis=-2)
     first = jnp.concatenate([block[..., :SWEEPS], edge[..., :SWEEPS]], axis=-2)
     final = jnp.concatenate([block[..., cols - SWEEPS :], edge[..., cols - SWEEPS :]], axis=-2)
-    right = shift(first, "col", -1)
-    left = shift(final, "col", 1)
+    right = jnp.swapaxes(shift(jnp.swapaxes(first, -1, -2), "col", -1), -1, -2)
+    left = jnp.swapaxes(shift(jnp.swapaxes(final, -1, -2), "col", 1), -1, -2)
     gap = jnp.zeros(right.shape[:-1] + (LANES - 2 * SWEEPS,), jnp.float32)
     side = jnp.concatenate([right, gap, left], axis=-1)
     return edge, side

time: 148 us -> 148 us (level)
  no operation moved by 1% of the time
where the time goes in v2:
time: 148 us; the launch traced here: 147 us
  Pallas kernels  54.9 us (37%)
  starting transfers between devices  39.6 us (27%)
  waiting for transfers between devices  39.6 us (27%)
  local copies, waits for them, and re-layouts  5.73 us (4%)
  other arithmetic  5.66 us (4%)
    ppermute x8, waiting for transfers between devices, shift(): return lax.ppermute(x, axis, pairs)  28.7 us
    ppermute x8, starting transfers between devices, shift(): return lax.ppermute(x, axis, pairs)  21.2 us
    pallas_call x1, Pallas kernels, on_device(): pl.pallas_call(functools.partial(factor_kernel, layers, 32), grid=(owned...  18 us
    pallas_call x1, Pallas kernels, on_device(): pl.pallas_call(functools.partial(saturation_kernel, layers), grid=(owned...  14.1 us
    all_to_all x1, starting transfers between devices, on_device(): lax.all_to_all(answer, ('row', 'col'), split_axis=0, concat_axis=0, tiled...  12.3 us
    all_to_all x1, waiting for transfers between devices, on_device(): lax.all_to_all(answer, ('row', 'col'), split_axis=0, concat_axis=0, tiled...  10.9 us
    pallas_call x1, Pallas kernels, on_device(): pl.pallas_call(functools.partial(owner_kernel, peers, per_peer), out_shap...  7.77 us
    pallas_call x1, Pallas kernels, on_device(): pl.pallas_call(relax_kernel, out_shape=f32(tile_rows, tile_cols), in_spec...  6.39 us
  transfers between devices with their start and end apart: 10, of which 6 were waited for; matrix products, arithmetic and copies ran while one was open for 3% of the time, Pallas kernels for 22%

profile of v2, /device:TPU:12, one launch (start us, length us, event | category | flops | bytes accessed | tf_op | source)
XLA Modules:
  0.0 147.3 jit_solution(12204205610017621788)
XLA Ops:
  4.7 5.2 %shard_map.87 = f32[32,136,128]{2,1,0:T(8,128)} custom-call(s32[2048]{0:T(1024)} %reshape.75.src, f32[32,128]{1,0:T(8,128)} %pad.4.labels, f32[256,512]{1,0:T(8,128)} %precip.1, f32[256,512]{1,0:T(8,128)} %head.3, s32[256,512]{1,0:T(8,128)} %land.3), custom_call_target="tpu_custom_call" | custom-call | tf_op jit(solution)/shard_map/pallas_call | solution.py:311
  10.0 6.0 %all-to-all-start = ((f32[32,136,128]{2,1,0:T(8,128)}), f32[32,136,128]{2,1,0:T(8,128)}, u32[]{:S(2)}, u32[]{:S(2)}) async-start(f32[32,136,128]{2,1,0:T(8,128)} %shard_map.87), calls=%async_computation | async-start | bytes 4456448 | tf_op jit(solution)/shard_map/all_to_all | solution.py:318
  16.5 2.2 %collective-permute-start = (f32[3,4,512]{2,1,0:T(4,128)S(1)}, f32[3,4,512]{2,1,0:T(4,128)S(1)}, u32[]{:S(2)}, u32[]{:S(2)}) collective-permute-start(f32[3,4,512]{2,1,0:T(4,128)S(1)} %get-tuple-element.28), channel_id=1, source_target_pairs={{8,0},{16,8},{24,16},{9,1},{17,9},{25,17},{10,2},{18,10},{26,18},{... | collective-permute-start | bytes 73736 | tf_op jit(solution)/shard_map/ppermute | solution.py:261
  18.7 2.1 %collective-permute-start.1 = (f32[3,4,512]{2,1,0:T(4,128)S(1)}, f32[3,4,512]{2,1,0:T(4,128)S(1)}, u32[]{:S(2)}, u32[]{:S(2)}) collective-permute-start(f32[3,4,512]{2,1,0:T(4,128)S(1)} %get-tuple-element.29), channel_id=1, source_target_pairs={{0,8},{8,16},{16,24},{1,9},{9,17},{17,25},{2,10},{10,18},{18,26},{... | collective-permute-start | bytes 73736 | tf_op jit(solution)/shard_map/ppermute | solution.py:261
  21.1 18.0 %shard_map.86 = (f32[16,1024,128]{2,1,0:T(8,128)}, f32[16,1024,128]{2,1,0:T(8,128)}, f32[16,1024,128]{2,1,0:T(8,128)}, f32[1024,128]{1,0:T(8,128)}, f32[1024,128]{1,0:T(8,128)}, /*index=5*/f32[1024,128]{1,0:T(8,128)}) custom-call(f32[16384,128]{1,0:T(8,128)} %bitcast.24, f32[1024,128]{1,0:T(8,128)} %ksat.1), custom_call_target="tpu_custom_call" | custom-call | flops 104857600 | bytes 33554432 | tf_op jit(solution)/shard_map/pallas_call | solution.py:330
  39.2 3.4 %collective-permute-start.2 = (f32[3,4,264]{1,2,0:T(8,128)S(1)}, f32[3,4,264]{1,2,0:T(8,128)S(1)}, u32[]{:S(2)}, u32[]{:S(2)}) collective-permute-start(f32[3,4,264]{1,2,0:T(8,128)S(1)} %maximum_bitcast_fusion), channel_id=1, source_target_pairs={{1,0},{2,1},{3,2},{4,3},{5,4},{6,5},{7,6},{9,8},{10,9},{11,10},{12... | collective-permute-start | bytes 38024 | tf_op jit(solution)/shard_map/ppermute | solution.py:261
  42.6 2.5 %collective-permute-start.3 = (f32[3,4,264]{1,2,0:T(8,128)S(1)}, f32[3,4,264]{1,2,0:T(8,128)S(1)}, u32[]{:S(2)}, u32[]{:S(2)}) collective-permute-start(f32[3,4,264]{1,2,0:T(8,128)S(1)} %maximum_bitcast_fusion.1), channel_id=1, source_target_pairs={{0,1},{1,2},{2,3},{3,4},{4,5},{5,6},{6,7},{8,9},{9,10},{10,11},{11... | collective-permute-start | bytes 38024 | tf_op jit(solution)/shard_map/ppermute | solution.py:261
  45.7 13.7 %collective-permute-done.2 = f32[3,4,264]{1,2,0:T(8,128)S(1)} collective-permute-done((f32[3,4,264]{1,2,0:T(8,128)S(1)}, f32[3,4,264]{1,2,0:T(8,128)S(1)}, u32[]{:S(2)}, u32[]{:S(2)}) %collective-permute-start.2) | collective-permute-done | bytes 12704 | tf_op jit(solution)/shard_map/ppermute | solution.py:261
  59.4 8.0 %collective-permute-done.3 = f32[3,4,264]{1,2,0:T(8,128)S(1)} collective-permute-done((f32[3,4,264]{1,2,0:T(8,128)S(1)}, f32[3,4,264]{1,2,0:T(8,128)S(1)}, u32[]{:S(2)}, u32[]{:S(2)}) %collective-permute-start.3) | collective-permute-done | bytes 12704 | tf_op jit(solution)/shard_map/ppermute | solution.py:261
  67.3 1.0 pad_maximum_fusion.1.mid_c
  69.9 7.8 %shard_map.88 = (f32[32,64,128]{2,1,0:T(8,128)}, f32[1024,128]{1,0:T(8,128)}, f32[1024,128]{1,0:T(8,128)}) custom-call(s32[2048]{0:T(1024)} %convert_element_type.45.slots, f32[32,136,128]{2,1,0:T(8,128)} %all-to-all-done.arrived, f32[1024,128]{1,0:T(8,128)} %get-tuple-element.18.rec0, f32[1024,128]{1,0:T(8,128)} %get-tuple-element.19.rec_x, ...), custom_call_target="tpu_custom_call" | custom-call | tf_op jit(solution)/shard_map/pallas_call | solution.py:345
  77.7 12.3 %all-to-all-start.1 = ((f32[32,64,128]{2,1,0:T(8,128)}), f32[32,64,128]{2,1,0:T(8,128)S(1)}, u32[]{:S(2)}, u32[]{:S(2)}) async-start(f32[32,64,128]{2,1,0:T(8,128)} %get-tuple-element.23), calls=%async_computation.1 | async-start | bytes 2097152 | tf_op jit(solution)/shard_map/all_to_all | solution.py:352
  90.0 14.1 %shard_map.89 = f32[16384,128]{1,0:T(8,128)} custom-call(f32[16,1024,128]{2,1,0:T(8,128)} %get-tuple-element.14.s0, f32[16,1024,128]{2,1,0:T(8,128)} %get-tuple-element.15.sx, f32[16,1024,128]{2,1,0:T(8,128)} %get-tuple-element.16.sy, f32[1024,128]{1,0:T(8,128)} %get-tuple-element.21.infil, f32[1024,128]{1,0:T(8,128)} %get-tuple-element.22.sig), custom_call_target="tpu_custom_call" | custom-call | flops 8388608 | bytes 33554432 | tf_op jit(solution)/shard_map/pallas_call | solution.py:354
  104.1 10.9 %all-to-all-done.1 = f32[32,64,128]{2,1,0:T(8,128)S(1)} async-done(((f32[32,64,128]{2,1,0:T(8,128)}), f32[32,64,128]{2,1,0:T(8,128)S(1)}, u32[]{:S(2)}, u32[]{:S(2)}) %all-to-all-start.1) | async-done | bytes 1048608 | tf_op jit(solution)/shard_map/all_to_all | solution.py:352
  115.1 1.0 copy-done.3
  116.1 3.4 %shard_map.90.src = f32[256,512]{1,0:T(8,128)} custom-call(s32[1024]{0:T(1024)} %get-tuple-element.42.position, f32[2048,128]{1,0:T(8,128)} %bitcast.26, f32[256,512]{1,0:T(8,128)} %head.3, s32[256,512]{1,0:T(8,128)} %land.3), custom_call_target="tpu_custom_call" | custom-call | tf_op jit(solution)/shard_map/pallas_call | solution.py:367
  120.2 3.3 %collective-permute-start.4 = (f32[4,512]{1,0:T(4,128)S(1)}, f32[4,512]{1,0:T(4,128)S(1)}, u32[]{:S(2)}, u32[]{:S(2)}) collective-permute-start(f32[4,512]{1,0:T(4,128)S(1)} %get-tuple-element.32), channel_id=1, source_target_pairs={{8,0},{16,8},{24,16},{9,1},{17,9},{25,17},{10,2},{18,10},{26,18},{... | collective-permute-start | bytes 24584 | tf_op jit(solution)/shard_map/ppermute | solution.py:261
  123.5 1.9 %collective-permute-start.5 = (f32[4,512]{1,0:T(4,128)S(1)}, f32[4,512]{1,0:T(4,128)S(1)}, u32[]{:S(2)}, u32[]{:S(2)}) collective-permute-start(f32[4,512]{1,0:T(4,128)S(1)} %get-tuple-element.33), channel_id=1, source_target_pairs={{0,8},{8,16},{16,24},{1,9},{9,17},{17,25},{2,10},{10,18},{18,26},{... | collective-permute-start | bytes 24584 | tf_op jit(solution)/shard_map/ppermute | solution.py:261
  125.5 1.1 fusion.20
  126.5 2.0 %collective-permute-done.5 = f32[4,512]{1,0:T(4,128)S(1)} collective-permute-done((f32[4,512]{1,0:T(4,128)S(1)}, f32[4,512]{1,0:T(4,128)S(1)}, u32[]{:S(2)}, u32[]{:S(2)}) %collective-permute-start.5) | collective-permute-done | bytes 8224 | tf_op jit(solution)/shard_map/ppermute | solution.py:261
  128.6 3.7 %collective-permute-start.6 = (f32[4,264]{0,1:T(8,128)S(1)}, f32[4,264]{0,1:T(8,128)S(1)}, u32[]{:S(2)}, u32[]{:S(2)}) collective-permute-start(f32[4,264]{0,1:T(8,128)S(1)} %maximum_bitcast_fusion.2), channel_id=1, source_target_pairs={{1,0},{2,1},{3,2},{4,3},{5,4},{6,5},{7,6},{9,8},{10,9},{11,10},{12... | collective-permute-start | bytes 12680 | tf_op jit(solution)/shard_map/ppermute | solution.py:261
  132.3 2.1 %collective-permute-start.7 = (f32[4,264]{0,1:T(8,128)S(1)}, f32[4,264]{0,1:T(8,128)S(1)}, u32[]{:S(2)}, u32[]{:S(2)}) collective-permute-start(f32[4,264]{0,1:T(8,128)S(1)} %maximum_bitcast_fusion.3), channel_id=1, source_target_pairs={{0,1},{1,2},{2,3},{3,4},{4,5},{5,6},{6,7},{8,9},{9,10},{10,11},{11... | collective-permute-start | bytes 12680 | tf_op jit(solution)/shard_map/ppermute | solution.py:261
  135.5 4.6 %collective-permute-done.7 = f32[4,264]{0,1:T(8,128)S(1)} collective-permute-done((f32[4,264]{0,1:T(8,128)S(1)}, f32[4,264]{0,1:T(8,128)S(1)}, u32[]{:S(2)}, u32[]{:S(2)}) %collective-permute-start.7) | collective-permute-done | bytes 4256 | tf_op jit(solution)/shard_map/ppermute | solution.py:261
  140.9 6.4 %shard_map.91 = f32[256,512]{1,0:T(8,128)} custom-call(f32[256,512]{1,0:T(8,128)} %shard_map.90.src, f32[8,512]{1,0:T(8,128)} %pad_maximum_fusion.4.src_r, f32[264,128]{1,0:T(8,128)} %pad_maximum_fusion.2.src_c, f32[3,256,512]{2,1,0:T(8,128)} %copy-done, f32[3,8,512]{2,1,0:T(8,128)} %pad_maximum_fusion.3.mid_r, f32[3,264,128]{2,1,0:T(8,128)} %pad_maximum_fusion.1.mid_c), custom_call_target="tpu_custom_call" | custom-call | tf_op jit(solution)/shard_map/pallas_call | solution.py:377
  (43 shorter events, 9.7 us)
Async XLA Ops:
  10.0 6.1 %copy-start.1 = (s32[256,512]{1,0:T(8,128)S(1)}, s32[256,512]{1,0:T(8,128)}, u32[]{:S(2)}) copy-start(s32[256,512]{1,0:T(8,128)} %land.3) | copy-start | bytes 1572868
  10.0 6.1 %copy-start.2 = (f32[256,512]{1,0:T(8,128)S(1)}, f32[256,512]{1,0:T(8,128)}, u32[]{:S(2)}) copy-start(f32[256,512]{1,0:T(8,128)} %head.3) | copy-start | bytes 1572868
  10.0 6.1 %copy-start.4 = (f32[256,512]{1,0:T(8,128)S(1)}, f32[256,512]{1,0:T(8,128)}, u32[]{:S(2)}) copy-start(f32[256,512]{1,0:T(8,128)} %param.9) | copy-start | bytes 1572868
  10.0 58.3 %all-to-all-start = ((f32[32,136,128]{2,1,0:T(8,128)}), f32[32,136,128]{2,1,0:T(8,128)}, u32[]{:S(2)}, u32[]{:S(2)}) async-start(f32[32,136,128]{2,1,0:T(8,128)} %shard_map.87), calls=%async_computation | async-start | bytes 4456448 | tf_op jit(solution)/shard_map/all_to_all | solution.py:318
  16.4 22.6 %copy-start = (f32[3,256,512]{2,1,0:T(8,128)}, f32[3,256,512]{2,1,0:T(8,128)S(1)}, u32[]{:S(2)}) copy-start(f32[3,256,512]{2,1,0:T(8,128)S(1)} %pad_maximum_fusion.mid) | copy-start | bytes 4718596
  16.5 22.6 %collective-permute-start = (f32[3,4,512]{2,1,0:T(4,128)S(1)}, f32[3,4,512]{2,1,0:T(4,128)S(1)}, u32[]{:S(2)}, u32[]{:S(2)}) collective-permute-start(f32[3,4,512]{2,1,0:T(4,128)S(1)} %get-tuple-element.28), channel_id=1, source_target_pairs={{8,0},{16,8},{24,16},{9,1},{17,9},{25,17},{10,2},{18,10},{26,18},{... | collective-permute-start | bytes 73736 | tf_op jit(solution)/shard_map/ppermute | solution.py:261
  18.7 20.4 %collective-permute-start.1 = (f32[3,4,512]{2,1,0:T(4,128)S(1)}, f32[3,4,512]{2,1,0:T(4,128)S(1)}, u32[]{:S(2)}, u32[]{:S(2)}) collective-permute-start(f32[3,4,512]{2,1,0:T(4,128)S(1)} %get-tuple-element.29), channel_id=1, source_target_pairs={{0,8},{8,16},{16,24},{1,9},{9,17},{17,25},{2,10},{10,18},{18,26},{... | collective-permute-start | bytes 73736 | tf_op jit(solution)/shard_map/ppermute | solution.py:261
  39.2 20.2 %collective-permute-start.2 = (f32[3,4,264]{1,2,0:T(8,128)S(1)}, f32[3,4,264]{1,2,0:T(8,128)S(1)}, u32[]{:S(2)}, u32[]{:S(2)}) collective-permute-start(f32[3,4,264]{1,2,0:T(8,128)S(1)} %maximum_bitcast_fusion), channel_id=1, source_target_pairs={{1,0},{2,1},{3,2},{4,3},{5,4},{6,5},{7,6},{9,8},{10,9},{11,10},{12... | collective-permute-start | bytes 38024 | tf_op jit(solution)/shard_map/ppermute | solution.py:261
  42.6 24.8 %collective-permute-start.3 = (f32[3,4,264]{1,2,0:T(8,128)S(1)}, f32[3,4,264]{1,2,0:T(8,128)S(1)}, u32[]{:S(2)}, u32[]{:S(2)}) collective-permute-start(f32[3,4,264]{1,2,0:T(8,128)S(1)} %maximum_bitcast_fusion.1), channel_id=1, source_target_pairs={{0,1},{1,2},{2,3},{3,4},{4,5},{5,6},{6,7},{8,9},{9,10},{10,11},{11... | collective-permute-start | bytes 38024 | tf_op jit(solution)/shard_map/ppermute | solution.py:261
  77.7 37.4 %all-to-all-start.1 = ((f32[32,64,128]{2,1,0:T(8,128)}), f32[32,64,128]{2,1,0:T(8,128)S(1)}, u32[]{:S(2)}, u32[]{:S(2)}) async-start(f32[32,64,128]{2,1,0:T(8,128)} %get-tuple-element.23), calls=%async_computation.1 | async-start | bytes 2097152 | tf_op jit(solution)/shard_map/all_to_all | solution.py:352
  115.1 1.0 copy-start.3
  120.2 6.3 %collective-permute-start.4 = (f32[4,512]{1,0:T(4,128)S(1)}, f32[4,512]{1,0:T(4,128)S(1)}, u32[]{:S(2)}, u32[]{:S(2)}) collective-permute-start(f32[4,512]{1,0:T(4,128)S(1)} %get-tuple-element.32), channel_id=1, source_target_pairs={{8,0},{16,8},{24,16},{9,1},{17,9},{25,17},{10,2},{18,10},{26,18},{... | collective-permute-start | bytes 24584 | tf_op jit(solution)/shard_map/ppermute | solution.py:261
  123.5 5.0 %collective-permute-start.5 = (f32[4,512]{1,0:T(4,128)S(1)}, f32[4,512]{1,0:T(4,128)S(1)}, u32[]{:S(2)}, u32[]{:S(2)}) collective-permute-start(f32[4,512]{1,0:T(4,128)S(1)} %get-tuple-element.33), channel_id=1, source_target_pairs={{0,8},{8,16},{16,24},{1,9},{9,17},{17,25},{2,10},{10,18},{18,26},{... | collective-permute-start | bytes 24584 | tf_op jit(solution)/shard_map/ppermute | solution.py:261
  128.6 6.9 %collective-permute-start.6 = (f32[4,264]{0,1:T(8,128)S(1)}, f32[4,264]{0,1:T(8,128)S(1)}, u32[]{:S(2)}, u32[]{:S(2)}) collective-permute-start(f32[4,264]{0,1:T(8,128)S(1)} %maximum_bitcast_fusion.2), channel_id=1, source_target_pairs={{1,0},{2,1},{3,2},{4,3},{5,4},{6,5},{7,6},{9,8},{10,9},{11,10},{12... | collective-permute-start | bytes 12680 | tf_op jit(solution)/shard_map/ppermute | solution.py:261
  132.3 7.8 %collective-permute-start.7 = (f32[4,264]{0,1:T(8,128)S(1)}, f32[4,264]{0,1:T(8,128)S(1)}, u32[]{:S(2)}, u32[]{:S(2)}) collective-permute-start(f32[4,264]{0,1:T(8,128)S(1)} %maximum_bitcast_fusion.3), channel_id=1, source_target_pairs={{0,1},{1,2},{2,3},{3,4},{4,5},{5,6},{6,7},{8,9},{9,10},{10,11},{11... | collective-permute-start | bytes 12680 | tf_op jit(solution)/shard_map/ppermute | solution.py:261
